TPU v7x, 32 devices: a whole 2x2x4 slice. The times are simulated.
32 devices in a mesh: leaf: 16 (over z, y, x), col: 2 (over core).
Axes of the slice: x: 2, y: 2, z: 4, core: 2. Of those that a mesh axis runs over, the one named last changes fastest.
Arguments:
- sources: bfloat16 [65536, 256], P('leaf', 'col'), may hold values from -6 to 6
- near_tiles: bfloat16 [256, 8, 256, 256], P('leaf', 'col'), may hold values from -0.125 to 0.125
- near_index: int32 [256, 8], P('leaf'), may hold values from 0 to 255, as said below
- near_count: int32 [256], P('leaf'), may hold values from 1 to 8, as said below
- leaf_basis: bfloat16 [256, 64, 256], P('leaf'), may hold values from -0.375 to 0.375
- leaf_coupling: bfloat16 [256, 64, 256], P('leaf'), may hold values from -0.375 to 0.375
- leaf_far: int32 [256, 4], P('leaf'), may hold values from 0 to 255, as said below
- up_leaf: bfloat16 [32, 64, 512], P('leaf'), may hold values from -0.25 to 0.25
- mid_coupling: bfloat16 [32, 64, 256], P('leaf'), may hold values from -0.375 to 0.375
- mid_far: int32 [32, 4], P('leaf'), may hold values from 0 to 31, as said below
- up_mid: bfloat16 [32, 64, 64], P('leaf'), may hold values from -0.75 to 0.75
- top_coupling: bfloat16 [4, 64, 256], replicated, may hold values from -0.4375 to 0.4375
Outputs:
- product: float32 [65536, 256], P('leaf', 'col')
Inputs may be any that keep to these rules, and one draw needn't show every extreme that they name: `near_index`: entry 0 of row i is i; the other 7 entries are distinct leaves j with j != i and |i - j| <= 8. Only the first near_count[i] slots of leaf i count; some leaf has all 8. `leaf_far`: row i holds 4 distinct leaves j != i with |i // 8 - j // 8| <= 1. `mid_far`: row a holds 4 distinct middle clusters b != a with |a // 8 - b // 8| <= 1.
All inputs are finite; a program needn't handle non-finite values.
Results may differ from a plain program's by a relative error of at most 0.01.
Values may be sent and summed in bfloat16 or wider, within the bound.
No kernel may reach another device: no remote copies, remote signals or barrier semaphores. Data moves between devices by JAX's collectives and lax.ppermute only.
A program may use at most 128 MiB of HBM per device.

v0:
```python
import jax
import jax.numpy as jnp
from jax import lax
from jax.sharding import PartitionSpec as P

CHILD = 8
FAR = 4


def padded(x, sides, width):
    for axis, dim in sides:
        size, length = (lax.axis_size(axis), x.shape[dim])
        up = [(i, (i + 1) % size) for i in range(size - 1)]
        down = [(j, i) for i, j in up]
        last = lax.slice_in_dim(x, length - width, length, axis=dim)
        first = lax.slice_in_dim(x, 0, width, axis=dim)
        before = lax.ppermute(last, axis, up)
        after = lax.ppermute(first, axis, down)
        x = jnp.concatenate([before, x, after], axis=dim)
    return x


def shards(
    sources,
    near_tiles,
    near_index,
    near_count,
    leaf_basis,
    leaf_coupling,
    leaf_far,
    up_leaf,
    mid_coupling,
    mid_far,
    up_mid,
    top_coupling,
):
    f32 = jnp.float32
    bf16 = jnp.bfloat16
    leaf_count = leaf_basis.shape[0]
    rank_size = leaf_basis.shape[1]
    leaf_size = leaf_basis.shape[2]
    col_count = sources.shape[1]
    mid_count = leaf_count // CHILD
    total_top = top_coupling.shape[0]
    device = lax.axis_index("leaf")
    first_leaf = device * leaf_count
    first_mid = device * mid_count
    window = padded(sources, (("leaf", 0),), CHILD * leaf_size)
    near_local = near_index - (first_leaf - CHILD)
    all_tiles = lax.all_gather(near_tiles, "col", axis=1, tiled=True)
    slot_count = all_tiles.shape[1]
    blocks = window.reshape(-1, leaf_size, window.shape[1])
    picked = blocks[near_local]
    live_mask = jnp.arange(slot_count)[None, :] < near_count[:, None]
    picked = jnp.where(live_mask[:, :, None, None], picked, jnp.zeros((), bf16))
    result = jnp.einsum("lsij,lsjc->lic", all_tiles, picked, preferred_element_type=f32)
    near_part = result.reshape(leaf_count * leaf_size, window.shape[1])
    leaf_blocks = sources.reshape(leaf_count, leaf_size, col_count)
    leaf_coef = jnp.einsum(
        "lrk,lkc->lrc", leaf_basis, leaf_blocks, preferred_element_type=f32
    ).astype(bf16)
    mid_coef = jnp.einsum(
        "qrk,qkc->qrc",
        up_leaf,
        leaf_coef.reshape(mid_count, CHILD * rank_size, col_count),
        preferred_element_type=f32,
    ).astype(bf16)
    mid_lift = jnp.einsum("qrs,qsc->qrc", up_mid, mid_coef, preferred_element_type=f32).astype(bf16)
    parent = (first_mid + jnp.arange(mid_count)) // CHILD
    mid_flat = mid_far.reshape(-1)
    top_range = jnp.arange(total_top)
    coef_piece = lax.all_gather(mid_coef, "leaf", axis=0, tiled=True)
    lift_piece = lax.all_gather(mid_lift, "leaf", axis=0, tiled=True)
    global_ids = jnp.arange(coef_piece.shape[0])
    group_map = (top_range[:, None] == (global_ids // CHILD)[None, :]).astype(bf16)
    top_total = jnp.einsum("pk,krc->prc", group_map, lift_piece, preferred_element_type=f32)
    global_ids = jnp.arange(coef_piece.shape[0])
    pick_map = (mid_flat[:, None] == global_ids[None, :]).astype(bf16)
    mid_picked = jnp.einsum("ik,krc->irc", pick_map, coef_piece, preferred_element_type=f32)
    top_coef = top_total.astype(bf16)
    parent_rows = top_coupling[parent]
    keep_mask = top_range[None, :] != parent[:, None]
    stacked = jnp.where(keep_mask[:, :, None, None], top_coef[None], jnp.zeros((), bf16))
    top_field = jnp.einsum(
        "qrk,qkc->qrc",
        parent_rows,
        stacked.reshape(mid_count, total_top * rank_size, col_count),
        preferred_element_type=f32,
    ).astype(bf16)
    mid_chosen = mid_picked.astype(bf16).reshape(mid_count, FAR * rank_size, col_count)
    mid_field = (
        jnp.einsum("qrk,qkc->qrc", mid_coupling, mid_chosen, preferred_element_type=f32)
        + jnp.einsum("qrs,qrc->qsc", up_mid, top_field, preferred_element_type=f32)
    ).astype(bf16)
    leaf_window = padded(leaf_coef, (("leaf", 0),), CHILD)
    far_local = leaf_far - (first_leaf - CHILD)
    leaf_chosen = leaf_window[far_local].reshape(leaf_count, FAR * rank_size, col_count)
    down_part = jnp.einsum("qrs,qrc->qsc", up_leaf, mid_field, preferred_element_type=f32).reshape(
        leaf_count, rank_size, col_count
    )
    leaf_field = (
        jnp.einsum("lrk,lkc->lrc", leaf_coupling, leaf_chosen, preferred_element_type=f32)
        + down_part
    ).astype(bf16)
    far_part = jnp.einsum(
        "lrk,lrc->lkc", leaf_basis, leaf_field, preferred_element_type=f32
    ).reshape(leaf_count * leaf_size, col_count)
    return near_part + far_part


def solution(mesh):
    return jax.shard_map(
        shards,
        mesh=mesh,
        in_specs=(
            P("leaf", "col"),
            P("leaf", "col", None, None),
            P("leaf", None),
            P("leaf"),
            P("leaf", None, None),
            P("leaf", None, None),
            P("leaf", None),
            P("leaf", None, None),
            P("leaf", None, None),
            P("leaf", None),
            P("leaf", None, None),
            P(),
        ),
        out_specs=P("leaf", "col"),
        check_vma=False,
    )
```

profile of v0, /device:TPU:0, one launch (start us, length us, event | category | flops | bytes accessed | tf_op | source)
XLA Modules:
  0.0 168.7 jit_solution(13844385451105794318)
XLA Ops:
  6.5 0.0 copy-start
  6.5 0.0 copy-start.1
  6.5 0.0 all-gather.2.cloned.1.call-start
  6.5 0.7 all-gather.2.cloned.1.call-update
  7.3 0.0 copy-start.9
  7.3 0.0 copy-start.4
  7.3 0.0 copy-start.6
  7.3 0.0 copy-start.11
  7.3 0.0 copy-start.7
  7.3 0.0 copy-start.10
  7.3 0.0 copy-start.8
  7.3 0.0 copy-start.5
  7.3 0.2 copy-done
  7.6 0.3 copy-done.1
  7.9 0.3 convolution_convert_fusion
  8.3 4.9 %collective-permute-start.2 = (bf16[8,64,128]{2,1,0:T(8,128)(2,1)S(1)}, bf16[8,64,128]{2,1,0:T(8,128)(2,1)S(1)}, u32[]{:S(2)}, u32[]{:S(2)}) collective-permute-start(bf16[8,64,128]{2,1,0:T(8,128)(2,1)S(1)} %get-tuple-element.7), channel_id=1, source_target_pairs={{0,2},{2,4},{4,6},{6,8},{8,10},{10,12},{12,14},{14,16},{16,18},{18... | collective-permute-start | bytes 393224 | tf_op jit(solution)/shard_map/ppermute | solution.py:17
  13.2 1.3 collective-permute-start.3
  14.5 1.1 fusion.33
  15.5 5.4 %collective-permute-start = (bf16[2048,128]{1,0:T(8,128)(2,1)}, bf16[2048,128]{1,0:T(8,128)(2,1)}, u32[]{:S(2)}, u32[]{:S(2)}) collective-permute-start(bf16[2048,128]{1,0:T(8,128)(2,1)} %get-tuple-element.5), channel_id=1, source_target_pairs={{0,2},{2,4},{4,6},{6,8},{8,10},{10,12},{12,14},{14,16},{16,18},{18... | collective-permute-start | bytes 1572872 | tf_op jit(solution)/shard_map/ppermute | solution.py:17
  20.9 1.3 collective-permute-start.1
  22.2 0.0 copy-done.9
  22.2 0.1 copy.27
  22.3 0.1 reshape.160
  22.4 0.0 copy-done.4
  22.4 0.2 convolution_convert_fusion.5
  22.6 0.0 copy-done.6
  22.6 0.1 fusion.12
  22.7 0.0 copy-start.3
  22.7 57.8 %all_gather.11 = bf16[32,64,128]{2,1,0:T(8,128)(2,1)S(1)} all-gather(bf16[2,64,128]{2,1,0:T(8,128)(2,1)S(1)} %fusion.12), channel_id=1, replica_groups=mesh['leaf'=16,'col'=2] {'leaf'}, dimensions={0}, use_global_device_ids=true | all-gather | bytes 557056 | tf_op jit(solution)/shard_map/all_gather | solution.py:73
  80.5 0.4 convolution_convert_fusion.2
  80.9 0.1 iota_compare_fusion.3
  81.0 0.1 broadcast_in_dim.59
  81.1 0.1 broadcast_in_dim.60
  81.2 0.0 copy-done.11
  81.2 0.1 eq.28
  81.3 38.7 %all_gather.10 = bf16[32,64,128]{2,1,0:T(8,128)(2,1)S(1)} all-gather(bf16[2,64,128]{2,1,0:T(8,128)(2,1)S(1)} %bitcast.59), channel_id=1, replica_groups=mesh['leaf'=16,'col'=2] {'leaf'}, dimensions={0}, use_global_device_ids=true | all-gather | bytes 557056 | tf_op jit(solution)/shard_map/all_gather | solution.py:72
  119.9 0.4 convolution_convert_fusion.1
  120.4 0.0 copy-done.7
  120.4 0.6 gather_fusion.2
  121.0 0.0 copy-done.10
  121.0 0.1 iota_compare_fusion
  121.1 0.0 copy-done.8
  121.1 0.4 fusion.11
  121.5 0.0 copy-done.5
  121.5 0.4 convolution_bitcast_fusion.1
  121.9 0.1 copy.25
  122.0 0.1 reshape.152
  122.1 0.2 copy.33
  122.3 0.0 collective-permute-done.2
  122.3 0.0 collective-permute-done.3
  122.3 1.0 pad_maximum_fusion.1
  123.3 0.7 gather_fusion.1
  124.0 0.0 copy-done.3
  124.0 1.9 %fusion.9 = f32[16,128,256]{2,1,0:T(8,128)} fusion(bf16[16,64,256]{2,1,0:T(8,128)(2,1)S(1)} %copy-done, f32[16,64,128]{2,1,0:T(8,128)S(1)} %bitcast.57, bf16[16,64,256]{2,1,0:T(8,128)(2,1)S(1)} %copy-done.3, bf16[16,256,128]{2,1,0:T(8,128)(2,1)S(1)} %bitcast.56), kind=kOutput, calls=%fused_computation.15 | convolution fusion | flops 134479872 | bytes 4718592 | tf_op jit(solution)/shard_map/lrk,lrc->lkc/dot_general | solution.py:105
  126.0 0.0 collective-permute-done
  126.0 0.0 collective-permute-done.1
  126.0 1.7 pad_maximum_fusion
  127.6 6.6 %gather_fusion = bf16[128,256,128]{2,1,0:T(8,128)(2,1)} fusion(bf16[32,256,128]{2,1,0:T(8,128)(2,1)S(1)} %bitcast.52, s32[1024]{0:T(1024)S(1)} %pad_clamp_fusion.2), kind=kCustom, calls=%fused_computation | custom fusion | bytes 16777728 | tf_op jit(solution)/shard_map/gather | solution.py:53
  134.2 0.0 copy-start.2
  134.2 12.1 %copy.26 = bf16[128,256,128]{1,2,0:T(8,128)(2,1)} copy(bf16[128,256,128]{2,1,0:T(8,128)(2,1)} %gather_fusion) | data formatting | bytes 16777216 | tf_op jit(solution)/shard_map/gather | solution.py:53
  146.3 0.0 all-gather.2.cloned.1.call-done
  146.3 0.0 copy-done.2
  146.3 12.7 %fusion.4 = f32[16,256,128]{1,2,0:T(8,128)} fusion(f32[16,128,256]{2,1,0:T(8,128)S(1)} %copy-done.2, bf16[16,8,256,256]{3,2,1,0:T(8,128)(2,1)} %all-gather.2.cloned.1.call-done, bf16[16,8,256,128]{2,3,1,0:T(8,128)(2,1)} %bitcast.54, pred[16,8]{1,0:T(8,128)(4,1)S(1)} %iota_compare_fusion), kind=kOutput, calls=%fused_computation.9 | convolution fusion | flops 2152202240 | bytes 29360256 | tf_op jit(solution)/shard_map/lsij,lsjc->lic/dot_general | solution.py:56
  159.0 2.9 %copy.34 = f32[16,256,128]{2,1,0:T(8,128)} copy(f32[16,256,128]{1,2,0:T(8,128)} %fusion.4) | data formatting | bytes 4194304 | tf_op jit(solution)/shard_map/add | solution.py:108
  (11 shorter events, 0.1 us)
Async XLA Ops:
  6.5 1.0 copy-start
  6.5 1.4 copy-start.1
  6.5 139.8 %all-gather.2.cloned.1.call-start = ((), (), s32[]{:S(2)}) async-start(), calls=%async_computation | async-start | bytes 25165824 | tf_op jit(solution)/shard_map/all_gather | solution.py:50
  7.3 14.9 %copy-start.9 = (s32[16,4]{0,1:T(4,128)S(1)}, s32[16,4]{0,1:T(4,128)}, u32[]{:S(2)}) copy-start(s32[16,4]{0,1:T(4,128)} %param.18) | copy-start | bytes 772
  7.3 15.1 %copy-start.4 = (bf16[2,64,512]{2,1,0:T(8,128)(2,1)S(1)}, bf16[2,64,512]{2,1,0:T(8,128)(2,1)}, u32[]{:S(2)}) copy-start(bf16[2,64,512]{2,1,0:T(8,128)(2,1)} %param.19) | copy-start | bytes 393220
  7.3 15.3 %copy-start.6 = (bf16[2,64,64]{2,1,0:T(8,128)(2,1)S(1)}, bf16[2,64,64]{2,1,0:T(8,128)(2,1)}, u32[]{:S(2)}) copy-start(bf16[2,64,64]{2,1,0:T(8,128)(2,1)} %param.22) | copy-start | bytes 49156
  7.3 73.9 %copy-start.11 = (s32[2,4]{1,0:T(2,128)S(1)}, s32[2,4]{1,0:T(2,128)}, u32[]{:S(2)}) copy-start(s32[2,4]{1,0:T(2,128)} %param.21) | copy-start | bytes 100
  7.3 113.1 %copy-start.7 = (bf16[4,64,256]{2,1,0:T(8,128)(2,1)S(1)}, bf16[4,64,256]{2,1,0:T(8,128)(2,1)}, u32[]{:S(2)}) copy-start(bf16[4,64,256]{2,1,0:T(8,128)(2,1)} %param.23) | copy-start | bytes 393220
  7.3 113.7 %copy-start.10 = (s32[16]{0:T(128)S(1)}, s32[16]{0:T(128)}, u32[]{:S(2)}) copy-start(s32[16]{0:T(128)} %param.15) | copy-start | bytes 196
  7.3 113.7 %copy-start.8 = (s32[16,8]{0,1:T(8,128)S(1)}, s32[16,8]{0,1:T(8,128)}, u32[]{:S(2)}) copy-start(s32[16,8]{0,1:T(8,128)} %param.14) | copy-start | bytes 1540
  7.3 114.1 %copy-start.5 = (bf16[2,64,256]{2,1,0:T(8,128)(2,1)S(1)}, bf16[2,64,256]{2,1,0:T(8,128)(2,1)}, u32[]{:S(2)}) copy-start(bf16[2,64,256]{2,1,0:T(8,128)(2,1)} %param.20) | copy-start | bytes 196612
  8.3 114.0 %collective-permute-start.2 = (bf16[8,64,128]{2,1,0:T(8,128)(2,1)S(1)}, bf16[8,64,128]{2,1,0:T(8,128)(2,1)S(1)}, u32[]{:S(2)}, u32[]{:S(2)}) collective-permute-start(bf16[8,64,128]{2,1,0:T(8,128)(2,1)S(1)} %get-tuple-element.7), channel_id=1, source_target_pairs={{0,2},{2,4},{4,6},{6,8},{8,10},{10,12},{12,14},{14,16},{16,18},{18... | collective-permute-start | bytes 393224 | tf_op jit(solution)/shard_map/ppermute | solution.py:17
  13.2 109.1 %collective-permute-start.3 = (bf16[8,64,128]{2,1,0:T(8,128)(2,1)S(1)}, bf16[8,64,128]{2,1,0:T(8,128)(2,1)}, u32[]{:S(2)}, u32[]{:S(2)}) collective-permute-start(bf16[8,64,128]{2,1,0:T(8,128)(2,1)S(1)} %get-tuple-element.8), channel_id=1, source_target_pairs={{2,0},{4,2},{6,4},{8,6},{10,8},{12,10},{14,12},{16,14},{18,16},{20... | collective-permute-start | bytes 393224 | tf_op jit(solution)/shard_map/ppermute | solution.py:18
  15.5 110.4 %collective-permute-start = (bf16[2048,128]{1,0:T(8,128)(2,1)}, bf16[2048,128]{1,0:T(8,128)(2,1)}, u32[]{:S(2)}, u32[]{:S(2)}) collective-permute-start(bf16[2048,128]{1,0:T(8,128)(2,1)} %get-tuple-element.5), channel_id=1, source_target_pairs={{0,2},{2,4},{4,6},{6,8},{8,10},{10,12},{12,14},{14,16},{16,18},{18... | collective-permute-start | bytes 1572872 | tf_op jit(solution)/shard_map/ppermute | solution.py:17
  20.9 105.1 %collective-permute-start.1 = (bf16[2048,128]{1,0:T(8,128)(2,1)}, bf16[2048,128]{1,0:T(8,128)(2,1)}, u32[]{:S(2)}, u32[]{:S(2)}) collective-permute-start(bf16[2048,128]{1,0:T(8,128)(2,1)} %get-tuple-element.6), channel_id=1, source_target_pairs={{2,0},{4,2},{6,4},{8,6},{10,8},{12,10},{14,12},{16,14},{18,16},{20... | collective-permute-start | bytes 1572872 | tf_op jit(solution)/shard_map/ppermute | solution.py:18
  22.7 101.3 %copy-start.3 = (bf16[16,64,256]{2,1,0:T(8,128)(2,1)S(1)}, bf16[16,64,256]{2,1,0:T(8,128)(2,1)}, u32[]{:S(2)}) copy-start(bf16[16,64,256]{2,1,0:T(8,128)(2,1)} %param.17) | copy-start | bytes 1572868
  134.2 12.1 %copy-start.2 = (f32[16,128,256]{2,1,0:T(8,128)S(1)}, f32[16,128,256]{2,1,0:T(8,128)}, u32[]{:S(2)}) copy-start(f32[16,128,256]{2,1,0:T(8,128)} %fusion.9) | copy-start | bytes 6291460
Sparse Core Ops, SparseCore 0:
  8.9 32.7 all-gather.1
where the time goes:
time: 169 us
  blocking collectives  96.5 us (57%)
  local copies, waits for them, and re-layouts  25.4 us (15%)
  matrix products  16.8 us (10%)
  between operations  13.7 us (8%)
  starting transfers between devices  12.8 us (8%)
  other arithmetic  2.82 us (2%)
    all_gather x1, blocking collectives, shards(): lift_piece = lax.all_gather(mid_lift, 'leaf', axis=0, tiled=True)  57.8 us
    all_gather x1, blocking collectives, shards(): coef_piece = lax.all_gather(mid_coef, 'leaf', axis=0, tiled=True)  38.7 us
    gather x2, local copies, waits for them, and re-layouts, shards(): picked = blocks[near_local]  18.7 us
    dot_general x1, matrix products, shards(): jnp.einsum('lsij,lsjc->lic', all_tiles, picked, preferred_element_type=f32)  12.7 us
    ppermute x2, starting transfers between devices, padded(): before = lax.ppermute(last, axis, up)  10.2 us
  transfers between devices with their start and end apart: 5, of which 0 were waited for; matrix products, arithmetic and copies ran while one was open for 17% of the time, Pallas kernels for 0%

commit v1 on v0

--- a/solution.py
+++ b/solution.py
@@ -70,10 +70,23 @@
     mid_flat = mid_far.reshape(-1)
     top_range = jnp.arange(total_top)
     coef_piece = lax.all_gather(mid_coef, "leaf", axis=0, tiled=True)
-    lift_piece = lax.all_gather(mid_lift, "leaf", axis=0, tiled=True)
     global_ids = jnp.arange(coef_piece.shape[0])
     group_map = (top_range[:, None] == (global_ids // CHILD)[None, :]).astype(bf16)
-    top_total = jnp.einsum("pk,krc->prc", group_map, lift_piece, preferred_element_type=f32)
+    devices, index, width_2 = (lax.axis_size("leaf"), lax.axis_index("leaf"), mid_lift.shape[0])
+    right = [(i_2, (i_2 + 1) % devices) for i_2 in range(devices)]
+    carried, top_total = (mid_lift, None)
+    for step in range(devices):
+        coming = lax.ppermute(carried, "leaf", right) if step < devices - 1 else None
+        absorb = jnp.einsum(
+            "pk,krc->prc",
+            lax.dynamic_slice_in_dim(
+                group_map, (index - step) % devices * width_2, carried.shape[0], axis=1
+            ),
+            carried,
+            preferred_element_type=f32,
+        )
+        top_total = absorb if top_total is None else top_total + absorb
+        carried = coming
     global_ids = jnp.arange(coef_piece.shape[0])
     pick_map = (mid_flat[:, None] == global_ids[None, :]).astype(bf16)
     mid_picked = jnp.einsum("ik,krc->irc", pick_map, coef_piece, preferred_element_type=f32)

time: 169 us -> 239 us (1.41)
  waiting for transfers between devices: 0.72 us -> 97.6 us
  blocking collectives: 96.5 us -> 56 us
  matrix products: 16.8 us -> 23.4 us
  starting transfers between devices: 12.8 us -> 16 us
  local copies, waits for them, and re-layouts: 25.4 us -> 27.9 us
    ppermute x0 -> x15, waiting for transfers between devices: none -> 96.9 us  [shards(): lax.ppermute(carried, 'leaf', right)]
    all_gather x1 -> x0, blocking collectives: 57.8 us -> none  [shards(): lift_piece = lax.all_gather(mid_lift, 'leaf', axis=0, tiled=True)]
    all_gather x1, blocking collectives: 38.7 us -> 56 us  [shards(): coef_piece = lax.all_gather(mid_coef, 'leaf', axis=0, tiled=True)]
    dot_general x1 -> x16, matrix products: 0.4 us -> 5.34 us  [shards(): jnp.einsum('pk,krc->prc', lax.dynamic_slice_in_dim(group_map, (index - st...]
    ppermute x0 -> x15, starting transfers between devices: none -> 4.63 us  [shards(): lax.ppermute(carried, 'leaf', right)]
  transfers between devices with their start and end apart: 5 -> 20, of which waited for: 0 -> 14; matrix products, arithmetic and copies ran while one was open for 17% -> 16% of each run, Pallas kernels for 0% -> 0%
where the time goes in v1:
time: 239 us; the launch traced here: 238 us
  waiting for transfers between devices  97.6 us (41%)
  blocking collectives  56 us (23%)
  local copies, waits for them, and re-layouts  27.9 us (12%)
  matrix products  23.4 us (10%)
  starting transfers between devices  16 us (7%)
  between operations  14.1 us (6%)
  other arithmetic  2.97 us (1%)
    ppermute x15, waiting for transfers between devices, shards(): lax.ppermute(carried, 'leaf', right)  96.9 us
    all_gather x1, blocking collectives, shards(): coef_piece = lax.all_gather(mid_coef, 'leaf', axis=0, tiled=True)  56 us
    gather x2, local copies, waits for them, and re-layouts, shards(): picked = blocks[near_local]  18.7 us
    dot_general x1, matrix products, shards(): jnp.einsum('lsij,lsjc->lic', all_tiles, picked, preferred_element_type=f32)  12.7 us
    ppermute x2, starting transfers between devices, padded(): before = lax.ppermute(last, axis, up)  8.74 us
    dot_general x16, matrix products, shards(): jnp.einsum('pk,krc->prc', lax.dynamic_slice_in_dim(group_map, (index - st...  5.34 us
  transfers between devices with their start and end apart: 20, of which 14 were waited for; matrix products, arithmetic and copies ran while one was open for 16% of the time, Pallas kernels for 0%

profile of v1, /device:TPU:0, one launch (start us, length us, event | category | flops | bytes accessed | tf_op | source)
XLA Modules:
  0.0 237.9 jit_solution(7732027248855110284)
XLA Ops:
  6.6 0.7 all-gather.2.cloned.1.call-update
  7.3 0.3 copy-done
  7.6 0.3 copy-done.1
  7.9 0.3 convolution_convert_fusion
  8.3 0.2 convolution_convert_fusion.4
  8.4 0.1 fusion.13
  8.6 3.0 %collective-permute-start.4 = (bf16[2,64,128]{2,1,0:T(8,128)(2,1)S(1)}, bf16[2,64,128]{2,1,0:T(8,128)(2,1)S(1)}, u32[]{:S(2)}, u32[]{:S(2)}) collective-permute-start(bf16[2,64,128]{2,1,0:T(8,128)(2,1)S(1)} %fusion.13), channel_id=1, source_target_pairs={{0,2},{2,4},{4,6},{6,8},{8,10},{10,12},{12,14},{14,16},{16,18},{18... | collective-permute-start | bytes 98312 | tf_op jit(solution)/shard_map/ppermute | solution.py:79
  11.6 3.4 %collective-permute-start.2 = (bf16[8,64,128]{2,1,0:T(8,128)(2,1)S(1)}, bf16[8,64,128]{2,1,0:T(8,128)(2,1)S(1)}, u32[]{:S(2)}, u32[]{:S(2)}) collective-permute-start(bf16[8,64,128]{2,1,0:T(8,128)(2,1)S(1)} %get-tuple-element.7), channel_id=1, source_target_pairs={{0,2},{2,4},{4,6},{6,8},{8,10},{10,12},{12,14},{14,16},{16,18},{18... | collective-permute-start | bytes 393224 | tf_op jit(solution)/shard_map/ppermute | solution.py:17
  15.0 1.3 collective-permute-start.3
  16.3 1.0 fusion.79
  17.3 5.3 %collective-permute-start = (bf16[2048,128]{1,0:T(8,128)(2,1)}, bf16[2048,128]{1,0:T(8,128)(2,1)}, u32[]{:S(2)}, u32[]{:S(2)}) collective-permute-start(bf16[2048,128]{1,0:T(8,128)(2,1)} %get-tuple-element.5), channel_id=1, source_target_pairs={{0,2},{2,4},{4,6},{6,8},{8,10},{10,12},{12,14},{14,16},{16,18},{18... | collective-permute-start | bytes 1572872 | tf_op jit(solution)/shard_map/ppermute | solution.py:17
  22.7 1.3 collective-permute-start.1
  24.0 0.1 eq.135
  24.1 0.1 copy.59
  24.1 0.1 reshape.160
  24.3 0.1 reshape.152
  24.7 0.2 fusion.38
  25.0 56.0 %all_gather.7 = bf16[32,64,128]{2,1,0:T(8,128)(2,1)S(1)} all-gather(bf16[2,64,128]{2,1,0:T(8,128)(2,1)S(1)} %bitcast.104), channel_id=1, replica_groups=mesh['leaf'=16,'col'=2] {'leaf'}, dimensions={0}, use_global_device_ids=true | all-gather | bytes 557056 | tf_op jit(solution)/shard_map/all_gather | solution.py:72
  81.0 0.4 convolution_convert_fusion.1
  81.7 0.7 broadcast_in_dim.60
  82.4 0.7 copy.61
  83.1 1.2 gather_fusion.2
  84.3 1.6 collective-permute-start.5
  85.9 0.2 convolution_add_fusion.14
  86.1 5.6 %collective-permute-done.5 = bf16[2,64,128]{2,1,0:T(8,128)(2,1)S(1)} collective-permute-done((bf16[2,64,128]{2,1,0:T(8,128)(2,1)S(1)}, bf16[2,64,128]{2,1,0:T(8,128)(2,1)S(1)}, u32[]{:S(2)}, u32[]{:S(2)}) %collective-permute-start.5) | collective-permute-done | bytes 32800 | tf_op jit(solution)/shard_map/ppermute | solution.py:79
  91.8 0.2 convolution_add_fusion.13
  92.0 7.3 %collective-permute-done.6 = bf16[2,64,128]{2,1,0:T(8,128)(2,1)S(1)} collective-permute-done((bf16[2,64,128]{2,1,0:T(8,128)(2,1)S(1)}, bf16[2,64,128]{2,1,0:T(8,128)(2,1)S(1)}, u32[]{:S(2)}, u32[]{:S(2)}) %collective-permute-start.6) | collective-permute-done | bytes 32800 | tf_op jit(solution)/shard_map/ppermute | solution.py:79
  99.3 0.2 convolution_add_fusion.12
  99.5 7.4 %collective-permute-done.7 = bf16[2,64,128]{2,1,0:T(8,128)(2,1)} collective-permute-done((bf16[2,64,128]{2,1,0:T(8,128)(2,1)S(1)}, bf16[2,64,128]{2,1,0:T(8,128)(2,1)}, u32[]{:S(2)}, u32[]{:S(2)}) %collective-permute-start.7) | collective-permute-done | bytes 32800 | tf_op jit(solution)/shard_map/ppermute | solution.py:79
  106.9 1.0 convolution_add_fusion.11
  108.0 0.6 copy-done.6
  108.6 1.0 pad_maximum_fusion.1
  109.7 0.7 gather_fusion.1
  110.4 4.3 %collective-permute-done.8 = bf16[2,64,128]{2,1,0:T(8,128)(2,1)} collective-permute-done((bf16[2,64,128]{2,1,0:T(8,128)(2,1)}, bf16[2,64,128]{2,1,0:T(8,128)(2,1)}, u32[]{:S(2)}, u32[]{:S(2)}) %collective-permute-start.8) | collective-permute-done | bytes 32800 | tf_op jit(solution)/shard_map/ppermute | solution.py:79
  114.7 1.0 convolution_add_fusion.10
  115.8 6.7 %collective-permute-done.9 = bf16[2,64,128]{2,1,0:T(8,128)(2,1)S(1)} collective-permute-done((bf16[2,64,128]{2,1,0:T(8,128)(2,1)}, bf16[2,64,128]{2,1,0:T(8,128)(2,1)S(1)}, u32[]{:S(2)}, u32[]{:S(2)}) %collective-permute-start.9) | collective-permute-done | bytes 32800 | tf_op jit(solution)/shard_map/ppermute | solution.py:79
  122.5 0.2 convolution_add_fusion.9
  122.7 7.3 %collective-permute-done.10 = bf16[2,64,128]{2,1,0:T(8,128)(2,1)S(1)} collective-permute-done((bf16[2,64,128]{2,1,0:T(8,128)(2,1)S(1)}, bf16[2,64,128]{2,1,0:T(8,128)(2,1)S(1)}, u32[]{:S(2)}, u32[]{:S(2)}) %collective-permute-start.10) | collective-permute-done | bytes 32800 | tf_op jit(solution)/shard_map/ppermute | solution.py:79
  130.0 0.2 convolution_add_fusion.8
  130.2 7.3 %collective-permute-done.11 = bf16[2,64,128]{2,1,0:T(8,128)(2,1)S(1)} collective-permute-done((bf16[2,64,128]{2,1,0:T(8,128)(2,1)S(1)}, bf16[2,64,128]{2,1,0:T(8,128)(2,1)S(1)}, u32[]{:S(2)}, u32[]{:S(2)}) %collective-permute-start.11) | collective-permute-done | bytes 32800 | tf_op jit(solution)/shard_map/ppermute | solution.py:79
  137.5 0.2 convolution_add_fusion.7
  137.7 7.3 %collective-permute-done.12 = bf16[2,64,128]{2,1,0:T(8,128)(2,1)S(1)} collective-permute-done((bf16[2,64,128]{2,1,0:T(8,128)(2,1)S(1)}, bf16[2,64,128]{2,1,0:T(8,128)(2,1)S(1)}, u32[]{:S(2)}, u32[]{:S(2)}) %collective-permute-start.12) | collective-permute-done | bytes 32800 | tf_op jit(solution)/shard_map/ppermute | solution.py:79
  145.0 0.2 convolution_add_fusion.6
  145.2 7.3 %collective-permute-done.13 = bf16[2,64,128]{2,1,0:T(8,128)(2,1)S(1)} collective-permute-done((bf16[2,64,128]{2,1,0:T(8,128)(2,1)S(1)}, bf16[2,64,128]{2,1,0:T(8,128)(2,1)S(1)}, u32[]{:S(2)}, u32[]{:S(2)}) %collective-permute-start.13) | collective-permute-done | bytes 32800 | tf_op jit(solution)/shard_map/ppermute | solution.py:79
  152.5 0.2 convolution_add_fusion.5
  152.7 7.3 %collective-permute-done.14 = bf16[2,64,128]{2,1,0:T(8,128)(2,1)S(1)} collective-permute-done((bf16[2,64,128]{2,1,0:T(8,128)(2,1)S(1)}, bf16[2,64,128]{2,1,0:T(8,128)(2,1)S(1)}, u32[]{:S(2)}, u32[]{:S(2)}) %collective-permute-start.14) | collective-permute-done | bytes 32800 | tf_op jit(solution)/shard_map/ppermute | solution.py:79
  160.0 0.2 convolution_add_fusion.4
  160.3 7.5 %collective-permute-done.15 = bf16[2,64,128]{2,1,0:T(8,128)(2,1)S(1)} collective-permute-done((bf16[2,64,128]{2,1,0:T(8,128)(2,1)S(1)}, bf16[2,64,128]{2,1,0:T(8,128)(2,1)S(1)}, u32[]{:S(2)}, u32[]{:S(2)}) %collective-permute-start.15) | collective-permute-done | bytes 32800 | tf_op jit(solution)/shard_map/ppermute | solution.py:79
  167.8 0.2 convolution_add_fusion.3
  168.0 7.3 %collective-permute-done.16 = bf16[2,64,128]{2,1,0:T(8,128)(2,1)S(1)} collective-permute-done((bf16[2,64,128]{2,1,0:T(8,128)(2,1)S(1)}, bf16[2,64,128]{2,1,0:T(8,128)(2,1)S(1)}, u32[]{:S(2)}, u32[]{:S(2)}) %collective-permute-start.16) | collective-permute-done | bytes 32800 | tf_op jit(solution)/shard_map/ppermute | solution.py:79
  175.3 0.2 convolution_add_fusion.2
  175.5 7.3 %collective-permute-done.17 = bf16[2,64,128]{2,1,0:T(8,128)(2,1)S(1)} collective-permute-done((bf16[2,64,128]{2,1,0:T(8,128)(2,1)S(1)}, bf16[2,64,128]{2,1,0:T(8,128)(2,1)S(1)}, u32[]{:S(2)}, u32[]{:S(2)}) %collective-permute-start.17) | collective-permute-done | bytes 32800 | tf_op jit(solution)/shard_map/ppermute | solution.py:79
  182.8 0.2 convolution_add_fusion.1
  183.1 7.3 %collective-permute-done.18 = bf16[2,64,128]{2,1,0:T(8,128)(2,1)S(1)} collective-permute-done((bf16[2,64,128]{2,1,0:T(8,128)(2,1)S(1)}, bf16[2,64,128]{2,1,0:T(8,128)(2,1)S(1)}, u32[]{:S(2)}, u32[]{:S(2)}) %collective-permute-start.18) | collective-permute-done | bytes 32800 | tf_op jit(solution)/shard_map/ppermute | solution.py:79
  190.3 0.2 fusion.10
  190.6 1.2 fusion.12
  191.8 1.2 convolution_bitcast_fusion.1
  193.0 0.2 copy.80
  193.2 1.9 fusion.9
  195.2 1.7 pad_maximum_fusion
  196.8 6.6 %gather_fusion = bf16[128,256,128]{2,1,0:T(8,128)(2,1)} fusion(bf16[32,256,128]{2,1,0:T(8,128)(2,1)S(1)} %bitcast.97, s32[1024]{0:T(1024)S(1)} %pad_clamp_fusion.2), kind=kCustom, calls=%fused_computation | custom fusion | bytes 16777728 | tf_op jit(solution)/shard_map/gather | solution.py:53
  203.4 12.1 %copy.58 = bf16[128,256,128]{1,2,0:T(8,128)(2,1)} copy(bf16[128,256,128]{2,1,0:T(8,128)(2,1)} %gather_fusion) | data formatting | bytes 16777216 | tf_op jit(solution)/shard_map/gather | solution.py:53
  215.5 12.7 %fusion.4 = f32[16,256,128]{1,2,0:T(8,128)} fusion(f32[16,128,256]{2,1,0:T(8,128)S(1)} %copy-done.2, bf16[16,8,256,256]{3,2,1,0:T(8,128)(2,1)} %all-gather.2.cloned.1.call-done, bf16[16,8,256,128]{2,3,1,0:T(8,128)(2,1)} %bitcast.99, pred[16,8]{1,0:T(8,128)(4,1)S(1)} %iota_compare_fusion.1), kind=kOutput, calls=%fused_computation.9 | convolution fusion | flops 2152202240 | bytes 29360256 | tf_op jit(solution)/shard_map/lsij,lsjc->lic/dot_general | solution.py:56
  228.2 2.9 %copy.81 = f32[16,256,128]{2,1,0:T(8,128)} copy(f32[16,256,128]{1,2,0:T(8,128)} %fusion.4) | data formatting | bytes 4194304 | tf_op jit(solution)/shard_map/add | solution.py:121
  (62 shorter events, 0.6 us)
Async XLA Ops:
  6.5 1.0 copy-start
  6.5 1.4 copy-start.1
  6.5 1.7 copy-start.4
  6.5 1.9 copy-start.8
  6.5 208.9 %all-gather.2.cloned.1.call-start = ((), (), s32[]{:S(2)}) async-start(), calls=%async_computation | async-start | bytes 25165824 | tf_op jit(solution)/shard_map/all_gather | solution.py:50
  7.3 16.7 %copy-start.14 = (s32[2,4]{1,0:T(2,128)S(1)}, s32[2,4]{1,0:T(2,128)}, u32[]{:S(2)}) copy-start(s32[2,4]{1,0:T(2,128)} %param.21) | copy-start | bytes 100
  7.3 16.8 %copy-start.11 = (s32[16,4]{0,1:T(4,128)S(1)}, s32[16,4]{0,1:T(4,128)}, u32[]{:S(2)}) copy-start(s32[16,4]{0,1:T(4,128)} %param.18) | copy-start | bytes 772
  7.3 16.9 %copy-start.10 = (s32[16,8]{0,1:T(8,128)S(1)}, s32[16,8]{0,1:T(8,128)}, u32[]{:S(2)}) copy-start(s32[16,8]{0,1:T(8,128)} %param.14) | copy-start | bytes 1540
  7.3 17.3 %copy-start.13 = (s32[16]{0:T(128)S(1)}, s32[16]{0:T(128)}, u32[]{:S(2)}) copy-start(s32[16]{0:T(128)} %param.15) | copy-start | bytes 196
  7.3 75.8 %copy-start.9 = (bf16[4,64,256]{2,1,0:T(8,128)(2,1)S(1)}, bf16[4,64,256]{2,1,0:T(8,128)(2,1)}, u32[]{:S(2)}) copy-start(bf16[4,64,256]{2,1,0:T(8,128)(2,1)} %param.23) | copy-start | bytes 393220
  8.6 75.7 %collective-permute-start.4 = (bf16[2,64,128]{2,1,0:T(8,128)(2,1)S(1)}, bf16[2,64,128]{2,1,0:T(8,128)(2,1)S(1)}, u32[]{:S(2)}, u32[]{:S(2)}) collective-permute-start(bf16[2,64,128]{2,1,0:T(8,128)(2,1)S(1)} %fusion.13), channel_id=1, source_target_pairs={{0,2},{2,4},{4,6},{6,8},{8,10},{10,12},{12,14},{14,16},{16,18},{18... | collective-permute-start | bytes 98312 | tf_op jit(solution)/shard_map/ppermute | solution.py:79
  11.6 96.4 %collective-permute-start.2 = (bf16[8,64,128]{2,1,0:T(8,128)(2,1)S(1)}, bf16[8,64,128]{2,1,0:T(8,128)(2,1)S(1)}, u32[]{:S(2)}, u32[]{:S(2)}) collective-permute-start(bf16[8,64,128]{2,1,0:T(8,128)(2,1)S(1)} %get-tuple-element.7), channel_id=1, source_target_pairs={{0,2},{2,4},{4,6},{6,8},{8,10},{10,12},{12,14},{14,16},{16,18},{18... | collective-permute-start | bytes 393224 | tf_op jit(solution)/shard_map/ppermute | solution.py:17
  15.0 93.6 %collective-permute-start.3 = (bf16[8,64,128]{2,1,0:T(8,128)(2,1)S(1)}, bf16[8,64,128]{2,1,0:T(8,128)(2,1)}, u32[]{:S(2)}, u32[]{:S(2)}) collective-permute-start(bf16[8,64,128]{2,1,0:T(8,128)(2,1)S(1)} %get-tuple-element.8), channel_id=1, source_target_pairs={{2,0},{4,2},{6,4},{8,6},{10,8},{12,10},{14,12},{16,14},{18,16},{20... | collective-permute-start | bytes 393224 | tf_op jit(solution)/shard_map/ppermute | solution.py:18
  17.3 177.8 %collective-permute-start = (bf16[2048,128]{1,0:T(8,128)(2,1)}, bf16[2048,128]{1,0:T(8,128)(2,1)}, u32[]{:S(2)}, u32[]{:S(2)}) collective-permute-start(bf16[2048,128]{1,0:T(8,128)(2,1)} %get-tuple-element.5), channel_id=1, source_target_pairs={{0,2},{2,4},{4,6},{6,8},{8,10},{10,12},{12,14},{14,16},{16,18},{18... | collective-permute-start | bytes 1572872 | tf_op jit(solution)/shard_map/ppermute | solution.py:17
  22.7 172.5 %collective-permute-start.1 = (bf16[2048,128]{1,0:T(8,128)(2,1)}, bf16[2048,128]{1,0:T(8,128)(2,1)}, u32[]{:S(2)}, u32[]{:S(2)}) collective-permute-start(bf16[2048,128]{1,0:T(8,128)(2,1)} %get-tuple-element.6), channel_id=1, source_target_pairs={{2,0},{4,2},{6,4},{8,6},{10,8},{12,10},{14,12},{16,14},{18,16},{20... | collective-permute-start | bytes 1572872 | tf_op jit(solution)/shard_map/ppermute | solution.py:18
  84.3 7.5 %collective-permute-start.5 = (bf16[2,64,128]{2,1,0:T(8,128)(2,1)S(1)}, bf16[2,64,128]{2,1,0:T(8,128)(2,1)S(1)}, u32[]{:S(2)}, u32[]{:S(2)}) collective-permute-start(bf16[2,64,128]{2,1,0:T(8,128)(2,1)S(1)} %collective-permute-done.4), channel_id=1, source_target_pairs={{0,2},{2,4},{4,6},{6,8},{8,10},{10,12},{12,14},{14,16},{16,18},{18... | collective-permute-start | bytes 98312 | tf_op jit(solution)/shard_map/ppermute | solution.py:79
  91.8 7.5 %collective-permute-start.6 = (bf16[2,64,128]{2,1,0:T(8,128)(2,1)S(1)}, bf16[2,64,128]{2,1,0:T(8,128)(2,1)S(1)}, u32[]{:S(2)}, u32[]{:S(2)}) collective-permute-start(bf16[2,64,128]{2,1,0:T(8,128)(2,1)S(1)} %collective-permute-done.5), channel_id=1, source_target_pairs={{0,2},{2,4},{4,6},{6,8},{8,10},{10,12},{12,14},{14,16},{16,18},{18... | collective-permute-start | bytes 98312 | tf_op jit(solution)/shard_map/ppermute | solution.py:79
  99.3 7.6 %collective-permute-start.7 = (bf16[2,64,128]{2,1,0:T(8,128)(2,1)S(1)}, bf16[2,64,128]{2,1,0:T(8,128)(2,1)}, u32[]{:S(2)}, u32[]{:S(2)}) collective-permute-start(bf16[2,64,128]{2,1,0:T(8,128)(2,1)S(1)} %collective-permute-done.6), channel_id=1, source_target_pairs={{0,2},{2,4},{4,6},{6,8},{8,10},{10,12},{12,14},{14,16},{16,18},{18... | collective-permute-start | bytes 98312 | tf_op jit(solution)/shard_map/ppermute | solution.py:79
  106.9 7.8 %collective-permute-start.8 = (bf16[2,64,128]{2,1,0:T(8,128)(2,1)}, bf16[2,64,128]{2,1,0:T(8,128)(2,1)}, u32[]{:S(2)}, u32[]{:S(2)}) collective-permute-start(bf16[2,64,128]{2,1,0:T(8,128)(2,1)} %collective-permute-done.7), channel_id=1, source_target_pairs={{0,2},{2,4},{4,6},{6,8},{8,10},{10,12},{12,14},{14,16},{16,18},{18... | collective-permute-start | bytes 98312 | tf_op jit(solution)/shard_map/ppermute | solution.py:79
  107.9 82.7 %copy-start.7 = (bf16[2,64,256]{2,1,0:T(8,128)(2,1)S(1)}, bf16[2,64,256]{2,1,0:T(8,128)(2,1)}, u32[]{:S(2)}) copy-start(bf16[2,64,256]{2,1,0:T(8,128)(2,1)} %gather_fusion.2) | copy-start | bytes 196612
  107.9 85.3 %copy-start.3 = (bf16[16,64,256]{2,1,0:T(8,128)(2,1)S(1)}, bf16[16,64,256]{2,1,0:T(8,128)(2,1)}, u32[]{:S(2)}) copy-start(bf16[16,64,256]{2,1,0:T(8,128)(2,1)} %param.17) | copy-start | bytes 1572868
  108.0 0.6 copy-start.6
  108.6 82.0 %copy-start.12 = (pred[2,256]{1,0:T(4,128)(4,1)S(1)}, pred[2,256]{1,0:T(4,128)(4,1)}, u32[]{:S(2)}) copy-start(pred[2,256]{1,0:T(4,128)(4,1)} %broadcast_in_dim.60) | copy-start | bytes 1540
  109.7 82.1 %copy-start.5 = (bf16[8,64,128]{2,1,0:T(8,128)(2,1)S(1)}, bf16[8,64,128]{2,1,0:T(8,128)(2,1)}, u32[]{:S(2)}) copy-start(bf16[8,64,128]{2,1,0:T(8,128)(2,1)} %copy.61) | copy-start | bytes 393220
  114.7 7.7 %collective-permute-start.9 = (bf16[2,64,128]{2,1,0:T(8,128)(2,1)}, bf16[2,64,128]{2,1,0:T(8,128)(2,1)S(1)}, u32[]{:S(2)}, u32[]{:S(2)}) collective-permute-start(bf16[2,64,128]{2,1,0:T(8,128)(2,1)} %collective-permute-done.8), channel_id=1, source_target_pairs={{0,2},{2,4},{4,6},{6,8},{8,10},{10,12},{12,14},{14,16},{16,18},{18... | collective-permute-start | bytes 98312 | tf_op jit(solution)/shard_map/ppermute | solution.py:79
  122.4 7.5 %collective-permute-start.10 = (bf16[2,64,128]{2,1,0:T(8,128)(2,1)S(1)}, bf16[2,64,128]{2,1,0:T(8,128)(2,1)S(1)}, u32[]{:S(2)}, u32[]{:S(2)}) collective-permute-start(bf16[2,64,128]{2,1,0:T(8,128)(2,1)S(1)} %collective-permute-done.9), channel_id=1, source_target_pairs={{0,2},{2,4},{4,6},{6,8},{8,10},{10,12},{12,14},{14,16},{16,18},{18... | collective-permute-start | bytes 98312 | tf_op jit(solution)/shard_map/ppermute | solution.py:79
  130.0 7.5 %collective-permute-start.11 = (bf16[2,64,128]{2,1,0:T(8,128)(2,1)S(1)}, bf16[2,64,128]{2,1,0:T(8,128)(2,1)S(1)}, u32[]{:S(2)}, u32[]{:S(2)}) collective-permute-start(bf16[2,64,128]{2,1,0:T(8,128)(2,1)S(1)} %collective-permute-done.10), channel_id=1, source_target_pairs={{0,2},{2,4},{4,6},{6,8},{8,10},{10,12},{12,14},{14,16},{16,18},{18... | collective-permute-start | bytes 98312 | tf_op jit(solution)/shard_map/ppermute | solution.py:79
  137.5 7.5 %collective-permute-start.12 = (bf16[2,64,128]{2,1,0:T(8,128)(2,1)S(1)}, bf16[2,64,128]{2,1,0:T(8,128)(2,1)S(1)}, u32[]{:S(2)}, u32[]{:S(2)}) collective-permute-start(bf16[2,64,128]{2,1,0:T(8,128)(2,1)S(1)} %collective-permute-done.11), channel_id=1, source_target_pairs={{0,2},{2,4},{4,6},{6,8},{8,10},{10,12},{12,14},{14,16},{16,18},{18... | collective-permute-start | bytes 98312 | tf_op jit(solution)/shard_map/ppermute | solution.py:79
  145.0 7.5 %collective-permute-start.13 = (bf16[2,64,128]{2,1,0:T(8,128)(2,1)S(1)}, bf16[2,64,128]{2,1,0:T(8,128)(2,1)S(1)}, u32[]{:S(2)}, u32[]{:S(2)}) collective-permute-start(bf16[2,64,128]{2,1,0:T(8,128)(2,1)S(1)} %collective-permute-done.12), channel_id=1, source_target_pairs={{0,2},{2,4},{4,6},{6,8},{8,10},{10,12},{12,14},{14,16},{16,18},{18... | collective-permute-start | bytes 98312 | tf_op jit(solution)/shard_map/ppermute | solution.py:79
  152.5 7.5 %collective-permute-start.14 = (bf16[2,64,128]{2,1,0:T(8,128)(2,1)S(1)}, bf16[2,64,128]{2,1,0:T(8,128)(2,1)S(1)}, u32[]{:S(2)}, u32[]{:S(2)}) collective-permute-start(bf16[2,64,128]{2,1,0:T(8,128)(2,1)S(1)} %collective-permute-done.13), channel_id=1, source_target_pairs={{0,2},{2,4},{4,6},{6,8},{8,10},{10,12},{12,14},{14,16},{16,18},{18... | collective-permute-start | bytes 98312 | tf_op jit(solution)/shard_map/ppermute | solution.py:79
  160.0 7.8 %collective-permute-start.15 = (bf16[2,64,128]{2,1,0:T(8,128)(2,1)S(1)}, bf16[2,64,128]{2,1,0:T(8,128)(2,1)S(1)}, u32[]{:S(2)}, u32[]{:S(2)}) collective-permute-start(bf16[2,64,128]{2,1,0:T(8,128)(2,1)S(1)} %collective-permute-done.14), channel_id=1, source_target_pairs={{0,2},{2,4},{4,6},{6,8},{8,10},{10,12},{12,14},{14,16},{16,18},{18... | collective-permute-start | bytes 98312 | tf_op jit(solution)/shard_map/ppermute | solution.py:79
  167.8 7.5 %collective-permute-start.16 = (bf16[2,64,128]{2,1,0:T(8,128)(2,1)S(1)}, bf16[2,64,128]{2,1,0:T(8,128)(2,1)S(1)}, u32[]{:S(2)}, u32[]{:S(2)}) collective-permute-start(bf16[2,64,128]{2,1,0:T(8,128)(2,1)S(1)} %collective-permute-done.15), channel_id=1, source_target_pairs={{0,2},{2,4},{4,6},{6,8},{8,10},{10,12},{12,14},{14,16},{16,18},{18... | collective-permute-start | bytes 98312 | tf_op jit(solution)/shard_map/ppermute | solution.py:79
  175.3 7.5 %collective-permute-start.17 = (bf16[2,64,128]{2,1,0:T(8,128)(2,1)S(1)}, bf16[2,64,128]{2,1,0:T(8,128)(2,1)S(1)}, u32[]{:S(2)}, u32[]{:S(2)}) collective-permute-start(bf16[2,64,128]{2,1,0:T(8,128)(2,1)S(1)} %collective-permute-done.16), channel_id=1, source_target_pairs={{0,2},{2,4},{4,6},{6,8},{8,10},{10,12},{12,14},{14,16},{16,18},{18... | collective-permute-start | bytes 98312 | tf_op jit(solution)/shard_map/ppermute | solution.py:79
  182.8 7.5 %collective-permute-start.18 = (bf16[2,64,128]{2,1,0:T(8,128)(2,1)S(1)}, bf16[2,64,128]{2,1,0:T(8,128)(2,1)S(1)}, u32[]{:S(2)}, u32[]{:S(2)}) collective-permute-start(bf16[2,64,128]{2,1,0:T(8,128)(2,1)S(1)} %collective-permute-done.17), channel_id=1, source_target_pairs={{0,2},{2,4},{4,6},{6,8},{8,10},{10,12},{12,14},{14,16},{16,18},{18... | collective-permute-start | bytes 98312 | tf_op jit(solution)/shard_map/ppermute | solution.py:79
  203.4 12.1 %copy-start.2 = (f32[16,128,256]{2,1,0:T(8,128)S(1)}, f32[16,128,256]{2,1,0:T(8,128)}, u32[]{:S(2)}) copy-start(f32[16,128,256]{2,1,0:T(8,128)} %fusion.9) | copy-start | bytes 6291460
Sparse Core Ops, SparseCore 0:
  8.9 32.7 all-gather.1
